TPU v7x, 32 devices: a whole 2x2x4 slice. The times are simulated.
32 devices in a mesh: doc: 4 (over y, x), seq: 8 (over z, core).
Axes of the slice: x: 2, y: 2, z: 4, core: 2. Of those that a mesh axis runs over, the one named last changes fastest.
Arguments:
- queries: bfloat16 [12288, 2048], P(('doc', 'seq')), parts along dimension 0, may hold values from -120 to 120
- keys: bfloat16 [12288, 2048], P(('doc', 'seq')), parts along dimension 0, may hold values from -4.1 to 4.1
- values: bfloat16 [12288, 2048], P(('doc', 'seq')), parts along dimension 0, may hold values from -6 to 6
- global_positions: int32 [256], P('doc'), parts along dimension 0, may hold values from 0 to 3070, as said below
- score_weight: float32 [2048], replicated, may hold values from -0.125 to 0.125
Outputs:
- token_scores: float32 [12288], P(('doc', 'seq')), parts along dimension 0
There are 4 independent parts, one for each index of `doc`. A program takes and returns all parts, laid end to end along the dimension named above; an argument that names none is the same for every part. Nothing has to cross between parts.
Inputs may be any that keep to these rules, and one draw needn't show every extreme that they name: `global_positions`: 64 distinct positions in increasing order; the first is 0 and the last is 3070.
All inputs are finite; a program needn't handle non-finite values.
Results may differ from a plain program's by a relative error of at most 0.0023.
Values may be sent and summed in bfloat16 or wider, within the bound.
No kernel may reach another device: no remote copies, remote signals or barrier semaphores. Data moves between devices by JAX's collectives and lax.ppermute only.
A program may use at most 64 MiB of HBM per device.

v0:
```python
import jax
import jax.numpy as jnp
from jax import lax
from jax.sharding import PartitionSpec as P

HEADS = 16
BLK = 64


def extended(block, sides, width):
    for axis, dim in sides:
        count = lax.axis_size(axis)
        forward = [(i, i + 1) for i in range(count - 1)]
        backward = [(target, source) for source, target in forward]
        low = lax.ppermute(
            lax.slice_in_dim(block, block.shape[dim] - width, None, axis=dim), axis, forward
        )
        high = lax.ppermute(lax.slice_in_dim(block, 0, width, axis=dim), axis, backward)
        block = jnp.concatenate([low, block, high], axis=dim)
    return block


def token_score(attended, score_weight):
    mean_square = jnp.mean(attended * attended, axis=-1)
    return jnp.sum(attended * score_weight, axis=-1) * lax.rsqrt(mean_square + 1e-06)


def on_device(queries, keys, values, global_positions, score_weight):
    row_count, model_width = queries.shape
    head_count = HEADS
    head_size = model_width // head_count
    block_rows = BLK
    local_blocks = row_count // block_rows
    glob_count = global_positions.shape[0]
    seq_index = lax.axis_index("seq")
    seq_count = lax.axis_size("seq")
    block_total = local_blocks * seq_count
    score_scale = head_size ** (-0.5)
    row_ids = seq_index * row_count + jnp.arange(row_count, dtype=jnp.int32)
    selected = global_positions[:, None] == row_ids[None, :]
    select_mat = selected.astype(jnp.bfloat16)
    glob_parts = (
        jnp.dot(select_mat, queries, preferred_element_type=jnp.float32).astype(jnp.bfloat16),
        jnp.dot(select_mat, keys, preferred_element_type=jnp.float32).astype(jnp.bfloat16),
        jnp.dot(select_mat, values, preferred_element_type=jnp.float32).astype(jnp.bfloat16),
    )
    glob_q, glob_k, glob_v = (
        lax.psum(glob_parts[0], "seq").astype(jnp.float32),
        lax.psum(glob_parts[1], "seq").astype(jnp.float32),
        lax.psum(glob_parts[2], "seq").astype(jnp.float32),
    )
    glob_q = glob_q.astype(jnp.bfloat16).reshape(glob_count, head_count, head_size)
    glob_k = glob_k.astype(jnp.bfloat16).reshape(glob_count, head_count, head_size)
    glob_v = glob_v.astype(jnp.bfloat16).reshape(glob_count, head_count, head_size)
    glob_block = global_positions // block_rows
    joined = jnp.concatenate((keys, values), axis=1)
    padded = extended(joined, (("seq", 0),), block_rows)
    padded = padded.reshape(local_blocks + 2, block_rows, 2, head_count, head_size)
    key_pad = padded[:, :, 0]
    value_pad = padded[:, :, 1]
    query_blocks = queries.reshape(local_blocks, block_rows, head_count, head_size)
    block_ids = seq_index * local_blocks + jnp.arange(local_blocks, dtype=jnp.int32)
    score_list = []
    valid_list = []
    for offset in range(3):
        score_list.append(
            jnp.einsum(
                "nqhd,nkhd->nhqk",
                query_blocks,
                key_pad[offset : offset + local_blocks],
                preferred_element_type=jnp.float32,
            )
        )
        key_block = block_ids + (offset - 1)
        in_range = (key_block >= 0) & (key_block < block_total)
        valid_list.append(jnp.broadcast_to(in_range[:, None], (local_blocks, block_rows)))
    score_list.append(
        jnp.einsum("nqhd,ghd->nhqg", query_blocks, glob_k, preferred_element_type=jnp.float32)
    )
    valid_list.append(jnp.abs(glob_block[None, :] - block_ids[:, None]) > 1)
    scores = jnp.concatenate(score_list, axis=-1) * score_scale
    key_valid = jnp.concatenate(valid_list, axis=-1)[:, None, None, :]
    scores = jnp.where(key_valid, scores, -jnp.inf)
    row_max = jnp.max(scores, axis=-1, keepdims=True)
    exp_scores = jnp.exp(scores - row_max)
    row_total = jnp.sum(exp_scores, axis=-1)
    weights = exp_scores.astype(jnp.bfloat16)
    mixture = jnp.einsum(
        "nhqg,ghd->nqhd", weights[..., 3 * block_rows :], glob_v, preferred_element_type=jnp.float32
    )
    for offset in range(3):
        mixture = mixture + jnp.einsum(
            "nhqk,nkhd->nqhd",
            weights[..., offset * block_rows : (offset + 1) * block_rows],
            value_pad[offset : offset + local_blocks],
            preferred_element_type=jnp.float32,
        )
    window_out = (mixture / jnp.transpose(row_total, (0, 2, 1))[..., None]).reshape(
        row_count, model_width
    )
    window_score = token_score(window_out, score_weight)
    local_keys = keys.reshape(row_count, head_count, head_size)
    local_values = values.reshape(row_count, head_count, head_size)
    glob_scores = (
        jnp.einsum("ghd,khd->hgk", glob_q, local_keys, preferred_element_type=jnp.float32)
        * score_scale
    )
    seg_max = jnp.max(glob_scores, axis=-1)
    glob_exp = jnp.exp(glob_scores - seg_max[..., None])
    seg_total = jnp.transpose(jnp.sum(glob_exp, axis=-1))
    seg_peak = jnp.transpose(seg_max)
    seg_acc = jnp.einsum(
        "hgk,khd->ghd",
        glob_exp.astype(jnp.bfloat16),
        local_values,
        preferred_element_type=jnp.float32,
    )
    top_peak = lax.pmax(seg_peak, "seq")
    rescale = jnp.exp(seg_peak - top_peak)
    scaled_acc = (seg_acc * rescale[..., None]).reshape(glob_count, model_width)
    acc_whole, total_whole = lax.psum((scaled_acc, seg_total * rescale), "seq")
    glob_out = (
        acc_whole.reshape(glob_count, head_count, head_size) / total_whole[:, :, None]
    ).reshape(glob_count, model_width)
    glob_score = token_score(glob_out, score_weight)
    placement = jnp.transpose(selected).astype(jnp.float32)
    is_global = jnp.any(selected, axis=0)
    placed = jnp.dot(placement, glob_score, precision=lax.Precision.HIGHEST)
    return jnp.where(is_global, placed, window_score)


def solution(mesh):
    placed = (
        P(("doc", "seq"), None),
        P(("doc", "seq"), None),
        P(("doc", "seq"), None),
        P("doc"),
        P(),
    )
    return jax.shard_map(
        on_device, mesh=mesh, in_specs=placed, out_specs=P(("doc", "seq")), check_vma=False
    )
```

profile of v0, /device:TPU:0, one launch (start us, length us, event | category | flops | bytes accessed | tf_op | source)
XLA Modules:
  0.0 179.3 jit_solution(5734152668019470307)
XLA Ops:
  6.5 0.0 all-reduce.6.cloned.1.call-start
  6.5 1.6 constant_dynamic-update-slice_fusion.1
  8.2 0.2 copy-done
  8.4 0.2 constant_dynamic-update-slice_fusion
  8.6 0.0 copy-start.3
  8.6 1.7 copy-done.3
  10.3 1.1 fusion.67
  11.3 3.2 %collective-permute-start = (bf16[64,4096]{1,0:T(8,128)(2,1)}, bf16[64,4096]{1,0:T(8,128)(2,1)}, u32[]{:S(2)}, u32[]{:S(2)}) collective-permute-start(bf16[64,4096]{1,0:T(8,128)(2,1)} %get-tuple-element.26), channel_id=1, source_target_pairs={{0,1},{1,2},{2,3},{3,4},{4,5},{5,6},{6,7},{8,9},{9,10},{10,11},{11... | collective-permute-start | bytes 1572872 | tf_op jit(solution)/shard_map/ppermute | solution.py:15
  14.5 1.3 collective-permute-start.1
  15.8 0.0 copy-done.1
  15.8 0.0 copy-done.9
  15.8 0.4 fusion.32
  16.2 0.0 copy-start.5
  16.3 0.4 fusion.31
  16.7 0.8 copy.163
  17.5 0.2 copy-done.5
  17.7 0.4 fusion.30
  18.1 0.9 copy_bitcast_fusion.13
  19.0 0.0 all-reduce.6.cloned.1.call-update
  19.1 0.0 all-reduce.4.cloned.1.call-start
  19.1 0.1 abs_compare_fusion
  19.2 1.8 %copy.102 = bf16[48,8,16,128]{3,2,1,0:T(8,128)(2,1)S(1)} copy(bf16[48,8,16,128]{3,1,2,0:T(8,128)(2,1)} %bitcast.131) | data formatting | bytes 3145728
  21.0 0.1 broadcast_in_dim.14
  21.1 0.1 broadcast_in_dim.16
  21.2 0.1 broadcast_in_dim.15
  21.3 0.1 pad_add_fusion
  21.3 0.1 compare_reduce_fusion
  21.4 59.4 %all-reduce.6.cloned.1.call-done = (bf16[64,16,128]{2,0,1:T(8,128)(2,1)}, bf16[64,16,128]{2,0,1:T(8,128)(2,1)}, bf16[64,16,128]{2,0,1:T(8,128)(2,1)}) async-done(((bf16[64,16,128]{2,0,1:T(8,128)(2,1)}, bf16[64,16,128]{2,0,1:T(8,128)(2,1)}, bf16[64,16,128]{2,0,1:T(8,128)(2,1)}), (bf16[64,16,128]{2,0,1:T(8,128)(2,1)}, bf16[64,16,128]{2,0,1:T(8,128)(2,1)}, ...) | async-done | bytes 786448 | tf_op jit(solution)/shard_map/psum | solution.py:48
  80.8 3.5 %fusion.68 = (f32[16,64]{1,0:T(8,128)S(1)}, f32[16,64,384]{2,1,0:T(8,128)}) fusion(bf16[64,16,128]{2,0,1:T(8,128)(2,1)} %get-tuple-element.9, bf16[384,2048]{1,0:T(8,128)(2,1)} %param.6), kind=kOutput, calls=%fused_computation.105 | convolution fusion | flops 101448704 | bytes 3411968 | tf_op jit(solution)/shard_map/ghd,khd->hgk/dot_general | solution.py:105
  84.3 13.9 %pmax.7 = f32[64,16]{0,1:T(8,128)S(1)} all-reduce(f32[64,16]{0,1:T(8,128)S(1)} %bitcast.135), channel_id=1, replica_groups=mesh['doc'=4,'seq'=8] {'seq'}, use_global_device_ids=true, to_apply=%region_3.4 | all-reduce | flops 1024 | bytes 8192 | tf_op jit(solution)/shard_map/pmax | solution.py:118
  98.2 0.0 copy-start.2
  98.2 2.0 %fusion.19 = f32[16,64]{1,0:T(8,128)S(1)} fusion(f32[16,64,384]{2,1,0:T(8,128)} %get-tuple-element.29, f32[16,64]{1,0:T(8,128)S(1)} %get-tuple-element.28), kind=kLoop, calls=%fused_computation.39 | loop fusion | flops 785408 | bytes 1581056 | tf_op jit(solution)/shard_map/reduce_sum | solution.py:110
  100.2 0.0 copy-done.2
  100.2 0.8 fusion.27
  101.0 0.0 copy-start.7
  101.0 0.8 copy.162
  101.9 0.0 all-reduce.4.cloned.1.call-update
  101.9 14.0 %psum.37 = f32[64,16]{0,1:T(8,128)S(1)} all-reduce(f32[64,16]{0,1:T(8,128)S(1)} %get-tuple-element.12), channel_id=1, replica_groups=mesh['doc'=4,'seq'=8] {'seq'}, use_global_device_ids=true, to_apply=%region_6.7 | all-reduce | flops 1024 | bytes 8192 | tf_op jit(solution)/shard_map/psum | solution.py:121
  116.0 0.1 copy.69
  116.0 0.0 copy-done.7
  116.1 0.6 convolution_bitcast_fusion
  116.6 0.0 collective-permute-done
  116.6 0.0 collective-permute-done.1
  116.6 1.3 copy-done.4
  118.0 1.4 maximum_bitcast_fusion
  119.3 1.2 copy.101
  120.6 2.1 %fusion.65 = (bf16[6,64,1,16,128]{4,3,2,1,0:T(8,128)(2,1)S(1)}, bf16[6,64,1,16,128]{4,3,2,1,0:T(8,128)(2,1)S(1)}, bf16[6,64,1,16,128]{4,3,2,1,0:T(8,128)(2,1)S(1...) fusion(bf16[8,64,2,16,128]{4,3,2,1,0:T(8,128)(2,1)S(1)} %bitcas, ...), kind=kLoop, calls=%fused_computation.102 | loop fusion | bytes 18874368 | tf_op jit(solution)/shard_map/slice | solution.py:95
  122.7 1.0 convolution_bitcast_fusion.1
  123.7 1.0 convolution_bitcast_fusion.2
  124.6 2.6 %convolution_bitcast_fusion.3 = f32[6,16,64,64]{3,2,1,0:T(8,128)} fusion(bf16[6,64,1,16,128]{4,3,2,1,0:T(8,128)(2,1)S(1)} %get-tuple-element.20, bf16[6,64,16,128]{3,2,1,0:T(8,128)(2,1)S(1)} %bitcast.130), kind=kOutput, calls=%fused_computation.17 | convolution fusion | flops 100663296 | bytes 4718592 | tf_op jit(solution)/shard_map/nqhd,nkhd->nhqk/dot_general | solution.py:67
  127.3 36.3 %fusion.64 = (f32[6,16,64]{2,1,0:T(8,128)S(1)}, bf16[6,16,64,256]{3,2,1,0:T(8,128)(2,1)S(1)}) fusion(f32[6,16,64,64]{3,2,1,0:T(8,128)S(1)} %convolution_bitcast_fusion, f32[6,16,64,64]{3,2,1,0:T(8,128)S(1)} %convolution_bitcast_fusion.1, f32[6,16,64,64]{3,2,1,0:T(8,128)S(1)} %convolution_bitcast_fusion.2, f32[6,16,64,64]{3,2,1,0:T(8,128)} %convolution_bitcast_fusion.3, ...), kind=kOutput, calls=%fused_computation.101 | output fusion | flops 12583167 | bytes 9463296 | tf_op jit(solution)/shard_map/sub | solution.py:85
  163.6 1.8 %fusion.66 = (bf16[6,16,64,64]{3,2,1,0:T(8,128)(2,1)S(1)}, bf16[6,16,64,64]{3,2,1,0:T(8,128)(2,1)S(1)}, bf16[6,16,64,64]{3,2,1,0:T(8,128)(2,1)S(1)}, bf16[6,16,64,64]{3,2,1,0:T(8,128)(2,1)S(1)}) fusion(bf16[6,16,64,256]{3,2,1,0:T(8,128)(2,1)S(1)} %get-tuple-element.15), kind=kLoop, calls=%fused_computation.103 | loop fusion | bytes 6291456 | tf_op jit(solution)/shard_map/slice | solution.py:94
  165.4 0.7 fusion.9
  166.1 0.0 copy-start.6
  166.1 0.7 fusion.10
  166.9 0.2 copy-done.6
  167.1 0.5 fusion.14
  167.6 0.1 copy-done.8
  167.8 2.1 %multiply_reduce_fusion = (f32[6,64]{1,0:T(8,128)S(1)}, f32[6,64]{1,0:T(8,128)S(1)}) fusion(f32[16,128]{1,0:T(8,128)S(1)} %bitcast.137, f32[6,64,16]{1,0,2:T(8,128)S(1)} %copy.86, bf16[6,64,1,16,128]{4,3,2,1,0:T(8,128)(2,1)S(1)} %get-tuple-element.16, bf16[6,16,64,64]{3,2,1,0:T(8,128)(2,1)S(1)} %get-tuple-element.22, f32[6,16,128,64]{2,3,0,1:T(8,128)S(1)} %fusion.9, ...), kind=kOutput, calls=%fused_computation.9 | convolution fusion | flops 106953984 | bytes 11832320 | tf_op jit(solution)/shard_map/nhqk,nkhd->nqhd/dot_general | solution.py:92
  169.9 0.1 mul.82
  170.0 0.2 div.43
  170.2 1.3 multiply_reduce_fusion.2
  171.5 0.3 convolution_reduce_fusion
  171.9 0.6 select_n.15
  (14 shorter events, 0.1 us)
Async XLA Ops:
  6.5 1.9 %copy-start = (bf16[384,2048]{1,0:T(8,128)(2,1)S(1)}, bf16[384,2048]{1,0:T(8,128)(2,1)}, u32[]{:S(2)}) copy-start(bf16[384,2048]{1,0:T(8,128)(2,1)} %param.7) | copy-start | bytes 4718596
  6.5 74.3 %all-reduce.6.cloned.1.call-start = ((), (), s32[]{:S(2)}) async-start(), calls=%async_computation.1 | async-start | bytes 1572864 | tf_op jit(solution)/shard_map/psum | solution.py:48
  8.6 1.7 copy-start.3
  10.3 5.5 %copy-start.1 = (bf16[384,2048]{1,0:T(8,128)(2,1)S(1)}, bf16[384,2048]{1,0:T(8,128)(2,1)}, u32[]{:S(2)}) copy-start(bf16[384,2048]{1,0:T(8,128)(2,1)} %param.6) | copy-start | bytes 4718596
  10.3 5.5 %copy-start.9 = (s32[64]{0:T(128)S(1)}, s32[64]{0:T(128)}, u32[]{:S(2)}) copy-start(s32[64]{0:T(128)} %param.8) | copy-start | bytes 772
  11.3 105.3 %collective-permute-start = (bf16[64,4096]{1,0:T(8,128)(2,1)}, bf16[64,4096]{1,0:T(8,128)(2,1)}, u32[]{:S(2)}, u32[]{:S(2)}) collective-permute-start(bf16[64,4096]{1,0:T(8,128)(2,1)} %get-tuple-element.26), channel_id=1, source_target_pairs={{0,1},{1,2},{2,3},{3,4},{4,5},{5,6},{6,7},{8,9},{9,10},{10,11},{11... | collective-permute-start | bytes 1572872 | tf_op jit(solution)/shard_map/ppermute | solution.py:15
  14.5 102.2 %collective-permute-start.1 = (bf16[64,4096]{1,0:T(8,128)(2,1)}, bf16[64,4096]{1,0:T(8,128)(2,1)}, u32[]{:S(2)}, u32[]{:S(2)}) collective-permute-start(bf16[64,4096]{1,0:T(8,128)(2,1)} %get-tuple-element.27), channel_id=1, source_target_pairs={{1,0},{2,1},{3,2},{4,3},{5,4},{6,5},{7,6},{9,8},{10,9},{11,10},{12... | collective-permute-start | bytes 1572872 | tf_op jit(solution)/shard_map/ppermute | solution.py:18
  16.2 1.4 copy-start.5
  19.1 150.9 %all-reduce.4.cloned.1.call-start = ((), (), s32[]{:S(2)}) async-start(), calls=%async_computation | async-start | bytes 1048576 | tf_op jit(solution)/shard_map/psum | solution.py:121
  98.2 2.0 %copy-start.2 = (f32[16,64,384]{2,1,0:T(8,128)S(1)}, f32[16,64,384]{2,1,0:T(8,128)}, u32[]{:S(2)}) copy-start(f32[16,64,384]{2,1,0:T(8,128)} %get-tuple-element.29) | copy-start | bytes 4718596
  101.0 15.0 %copy-start.7 = (bf16[64,16,128]{2,0,1:T(8,128)(2,1)S(1)}, bf16[64,16,128]{2,0,1:T(8,128)(2,1)}, u32[]{:S(2)}) copy-start(bf16[64,16,128]{2,0,1:T(8,128)(2,1)} %get-tuple-element.10) | copy-start | bytes 786436
  116.0 1.9 %copy-start.4 = (bf16[384,4096]{1,0:T(8,128)(2,1)S(1)}, bf16[384,4096]{1,0:T(8,128)(2,1)}, u32[]{:S(2)}) copy-start(bf16[384,4096]{1,0:T(8,128)(2,1)} %copy-done.3) | copy-start | bytes 9437188
  166.1 1.0 copy-start.6
  167.1 0.7 copy-start.8
Sparse Core Ops, SparseCore 0:
  19.2 61.5 all-reduce.5
  102.0 54.4 all-reduce.3
where the time goes:
time: 180 us; the launch traced here: 179 us
  waiting for transfers between devices  59.4 us (33%)
  other arithmetic  41.9 us (23%)
  blocking collectives  28 us (16%)
  local copies, waits for them, and re-layouts  16.8 us (9%)
  matrix products  15.1 us (8%)
  between operations  13.7 us (8%)
  starting transfers between devices  4.48 us (2%)
    psum x1, waiting for transfers between devices, on_device(): lax.psum(glob_parts[0], 'seq').astype(jnp.float32)  59.4 us
    sub x1, other arithmetic, on_device(): exp_scores = jnp.exp(scores - row_max)  36.3 us
    psum x1, blocking collectives, on_device(): acc_whole, total_whole = lax.psum((scaled_acc, seg_total * rescale), 'seq')  14 us
    pmax x1, blocking collectives, on_device(): top_peak = lax.pmax(seg_peak, 'seq')  13.9 us
    unnamed x23, local copies, waits for them, and re-layouts  8.46 us
    dot_general x3, matrix products, on_device(): jnp.einsum('nqhd,nkhd->nhqk', query_blocks, key_pad[offset:offset + local...  4.54 us
  transfers between devices with their start and end apart: 4, of which 1 were waited for; matrix products, arithmetic and copies ran while one was open for 36% of the time, Pallas kernels for 0%

commit v1 on v0

--- a/solution.py
+++ b/solution.py
@@ -45,7 +45,7 @@
         jnp.dot(select_mat, values, preferred_element_type=jnp.float32).astype(jnp.bfloat16),
     )
     glob_q, glob_k, glob_v = (
-        lax.psum(glob_parts[0], "seq").astype(jnp.float32),
+        jnp.sum(lax.all_gather(glob_parts[0], "seq"), axis=0).astype(jnp.float32),
         lax.psum(glob_parts[1], "seq").astype(jnp.float32),
         lax.psum(glob_parts[2], "seq").astype(jnp.float32),
     )

time: 180 us -> 226 us (1.26)
  waiting for transfers between devices: 59.4 us -> 91.5 us
  matrix products: 15.1 us -> 26.8 us
    psum x1, waiting for transfers between devices: 0.01 us -> 34.8 us  [on_device(): acc_whole, total_whole = lax.psum((scaled_acc, seg_total * rescale), 'seq')]
    dot_general x3, matrix products: 3.55 us -> 9.58 us  [on_device(): jnp.einsum('nhqk,nkhd->nqhd', weights[..., offset * block_rows:(offset +...]
    dot_general x1, matrix products: 0.56 us -> 3.37 us  [on_device(): jnp.einsum('nqhd,ghd->nhqg', query_blocks, glob_k, preferred_element_type...]
    psum x1, waiting for transfers between devices: 59.4 us -> 56.6 us  [on_device(): lax.psum(glob_parts[1], 'seq').astype(jnp.float32)]
    dot_general x1, matrix products: 3.47 us -> 0.91 us  [on_device(): jnp.einsum('ghd,khd->hgk', glob_q, local_keys, preferred_element_type=jnp...]
    unnamed x23 -> x29, local copies, waits for them, and re-layouts: 8.46 us -> 8.53 us
  transfers between devices with their start and end apart: 4 -> 5, of which waited for: 1 -> 2; matrix products, arithmetic and copies ran while one was open for 36% -> 32% of each run, Pallas kernels for 0% -> 0%
where the time goes in v1:
time: 226 us
  waiting for transfers between devices  91.5 us (40%)
  other arithmetic  43.5 us (19%)
  blocking collectives  28 us (12%)
  matrix products  26.8 us (12%)
  local copies, waits for them, and re-layouts  18 us (8%)
  between operations  13.4 us (6%)
  starting transfers between devices  4.54 us (2%)
    psum x1, waiting for transfers between devices, on_device(): lax.psum(glob_parts[1], 'seq').astype(jnp.float32)  56.6 us
    sub x1, other arithmetic, on_device(): exp_scores = jnp.exp(scores - row_max)  37.3 us
    psum x1, waiting for transfers between devices, on_device(): acc_whole, total_whole = lax.psum((scaled_acc, seg_total * rescale), 'seq')  34.8 us
    psum x1, blocking collectives, on_device(): acc_whole, total_whole = lax.psum((scaled_acc, seg_total * rescale), 'seq')  14.1 us
    pmax x1, blocking collectives, on_device(): top_peak = lax.pmax(seg_peak, 'seq')  13.9 us
    dot_general x3, matrix products, on_device(): jnp.einsum('nhqk,nkhd->nqhd', weights[..., offset * block_rows:(offset +...  9.58 us
    unnamed x29, local copies, waits for them, and re-layouts  8.53 us
    dot_general x3, matrix products, on_device(): jnp.einsum('nqhd,nkhd->nhqk', query_blocks, key_pad[offset:offset + local...  6.24 us
  transfers between devices with their start and end apart: 5, of which 2 were waited for; matrix products, arithmetic and copies ran while one was open for 32% of the time, Pallas kernels for 0%

profile of v1, /device:TPU:0, one launch (start us, length us, event | category | flops | bytes accessed | tf_op | source)
XLA Modules:
  0.0 225.7 jit_solution(2544254726674122142)
XLA Ops:
  6.5 0.0 all-reduce.6.cloned.1.call-start
  6.5 1.6 constant_dynamic-update-slice_fusion.1
  8.2 0.2 copy-done
  8.4 0.2 constant_dynamic-update-slice_fusion
  8.6 0.0 copy-start.4
  8.6 1.7 copy-done.4
  10.3 1.0 fusion.68
  11.3 3.2 %collective-permute-start = (bf16[64,4096]{1,0:T(8,128)(2,1)}, bf16[64,4096]{1,0:T(8,128)(2,1)}, u32[]{:S(2)}, u32[]{:S(2)}) collective-permute-start(bf16[64,4096]{1,0:T(8,128)(2,1)} %get-tuple-element.25), channel_id=1, source_target_pairs={{0,1},{1,2},{2,3},{3,4},{4,5},{5,6},{6,7},{8,9},{9,10},{10,11},{11... | collective-permute-start | bytes 1572872 | tf_op jit(solution)/shard_map/ppermute | solution.py:15
  14.5 1.3 collective-permute-start.1
  15.8 0.0 copy-done.1
  15.8 0.0 copy-done.12
  15.8 0.4 fusion.31
  16.2 0.0 copy-start.6
  16.3 0.4 fusion.30
  16.7 0.8 copy.167
  17.5 0.8 copy.168
  18.3 0.0 all-reduce.6.cloned.1.call-update
  18.3 0.0 all-gather.3.cloned.1.call-start
  18.3 1.1 convolution_convert_fusion.2
  19.5 0.0 all-gather.3.cloned.1.call-update
  19.5 0.0 all-reduce.4.cloned.1.call-start
  19.6 1.8 copy.101
  21.4 0.1 abs_compare_fusion
  21.5 0.1 broadcast_in_dim.15
  21.6 0.1 broadcast_in_dim.16
  21.7 0.1 broadcast_in_dim.14
  21.7 0.1 pad_add_fusion
  21.8 0.1 compare_reduce_fusion
  21.9 56.6 %all-reduce.6.cloned.1.call-done = (bf16[64,16,128]{2,0,1:T(8,128)(2,1)}, bf16[64,16,128]{2,0,1:T(8,128)(2,1)}) async-done(((bf16[64,16,128]{2,0,1:T(8,128)(2,1)}, bf16[64,16,128]{2,0,1:T(8,128)(2,1)}), (bf16[64,16,128]{2,0,1:T(8,128)(2,1)}, bf16[64,16,128]{2,0,1:T(8,128)(2,1)})) %all-reduce.6.cloned.1.call-update) | async-done | bytes 524304 | tf_op jit(solution)/shard_map/psum | solution.py:49
  78.5 3.4 %convolution_bitcast_fusion = f32[6,16,64,64]{3,2,1,0:T(8,128)} fusion(bf16[6,64,16,128]{3,2,1,0:T(8,128)(2,1)S(1)} %bitcast.133, bf16[64,16,128]{2,0,1:T(8,128)(2,1)} %get-tuple-element.9), kind=kOutput, calls=%fused_computation.14 | convolution fusion | flops 100663296 | bytes 3407872 | tf_op jit(solution)/shard_map/nqhd,ghd->nhqg/dot_general | solution.py:78
  81.9 0.0 collective-permute-done
  81.9 0.0 collective-permute-done.1
  81.9 1.4 maximum_bitcast_fusion
  83.3 1.3 copy.100
  84.6 2.6 %fusion.66 = (bf16[6,64,1,16,128]{4,3,2,1,0:T(8,128)(2,1)}, bf16[6,64,1,16,128]{4,3,2,1,0:T(8,128)(2,1)S(1)}, bf16[6,64,1,16,128]{4,3,2,1,0:T(8,128)(2,1)S(1)}, ...) fusion(bf16[8,64,2,16,128]{4,3,2,1,0:T(8,128)(2,1)S(1)} %bitcas, ...), kind=kLoop, calls=%fused_computation.102 | loop fusion | bytes 18874368 | tf_op jit(solution)/shard_map/slice | solution.py:95
  87.1 1.0 convolution_bitcast_fusion.2
  88.1 2.7 %convolution_bitcast_fusion.3 = f32[6,16,64,64]{3,2,1,0:T(8,128)} fusion(bf16[6,64,1,16,128]{4,3,2,1,0:T(8,128)(2,1)S(1)} %get-tuple-element.19, bf16[6,64,16,128]{3,2,1,0:T(8,128)(2,1)S(1)} %bitcast.135), kind=kOutput, calls=%fused_computation.17 | convolution fusion | flops 100663296 | bytes 4718592 | tf_op jit(solution)/shard_map/nqhd,nkhd->nhqk/dot_general | solution.py:67
  90.8 2.6 %convolution_bitcast_fusion.1 = f32[6,16,64,64]{3,2,1,0:T(8,128)} fusion(bf16[6,64,1,16,128]{4,3,2,1,0:T(8,128)(2,1)S(1)} %get-tuple-element.17, bf16[6,64,16,128]{3,2,1,0:T(8,128)(2,1)S(1)} %bitcast.136), kind=kOutput, calls=%fused_computation.15 | convolution fusion | flops 100663296 | bytes 4718592 | tf_op jit(solution)/shard_map/nqhd,nkhd->nhqk/dot_general | solution.py:67
  93.4 37.3 %fusion.65 = (f32[6,16,64]{2,1,0:T(8,128)S(1)}, bf16[6,16,64,256]{3,2,1,0:T(8,128)(2,1)S(1)}) fusion(f32[6,16,64,64]{3,2,1,0:T(8,128)S(1)} %copy-done.7, f32[6,16,64,64]{3,2,1,0:T(8,128)} %convolution_bitcast_fusion.1, f32[6,16,64,64]{3,2,1,0:T(8,128)S(1)} %convolution_bitcast_fusion.2, f32[6,16,64,64]{3,2,1,0:T(8,128)} %convolution_bitcast_fusion.3, ...), kind=kOutput, calls=%fused_computation.101 | output fusion | flops 12583167 | bytes 9463296 | tf_op jit(solution)/shard_map/sub | solution.py:85
  130.7 0.0 copy-start.10
  130.7 2.7 %fusion.67 = (bf16[6,16,64,64]{3,2,1,0:T(8,128)(2,1)}, bf16[6,16,64,64]{3,2,1,0:T(8,128)(2,1)S(1)}, bf16[6,16,64,64]{3,2,1,0:T(8,128)(2,1)S(1)}, bf16[6,16,64,64]{3,2,1,0:T(8,128)(2,1)S(1)}) fusion(bf16[6,16,64,256]{3,2,1,0:T(8,128)(2,1)S(1)} %get-tuple-element.14), kind=kLoop, calls=%fused_computation.103 | loop fusion | bytes 6291456 | tf_op jit(solution)/shard_map/slice | solution.py:94
  133.4 2.3 fusion.14
  135.6 2.4 %fusion.10 = f32[6,16,128,64]{2,3,0,1:T(8,128)} fusion(bf16[6,64,1,16,128]{4,3,2,1,0:T(8,128)(2,1)S(1)} %get-tuple-element.16, bf16[6,16,64,64]{3,2,1,0:T(8,128)(2,1)S(1)} %get-tuple-element.23), kind=kOutput, calls=%fused_computation.28 | convolution fusion | flops 100663296 | bytes 5505024 | tf_op jit(solution)/shard_map/nhqk,nkhd->nqhd/dot_general | solution.py:92
  138.0 2.4 %fusion.9 = f32[6,16,128,64]{2,3,0,1:T(8,128)} fusion(bf16[6,64,1,16,128]{4,3,2,1,0:T(8,128)(2,1)S(1)} %get-tuple-element.20, bf16[6,16,64,64]{3,2,1,0:T(8,128)(2,1)S(1)} %get-tuple-element.22), kind=kOutput, calls=%fused_computation.26 | convolution fusion | flops 100663296 | bytes 5505024 | tf_op jit(solution)/shard_map/nhqk,nkhd->nqhd/dot_general | solution.py:92
  140.4 2.1 reduce_sum.66
  142.5 0.9 fusion.69
  143.4 0.0 copy-start.3
  143.4 1.2 copy-done.3
  144.6 0.6 fusion.19
  145.2 13.9 %pmax.7 = f32[64,16]{0,1:T(8,128)S(1)} all-reduce(f32[64,16]{0,1:T(8,128)S(1)} %bitcast.143), channel_id=1, replica_groups=mesh['doc'=4,'seq'=8] {'seq'}, use_global_device_ids=true, to_apply=%region_3.4 | all-reduce | flops 1024 | bytes 8192 | tf_op jit(solution)/shard_map/pmax | solution.py:118
  159.1 2.1 fusion.27
  161.3 0.0 copy-start.11
  161.3 0.8 copy.166
  162.1 0.0 all-reduce.4.cloned.1.call-update
  162.2 0.7 copy-done.8
  162.9 4.8 %multiply_reduce_fusion = (f32[6,64]{1,0:T(8,128)S(1)}, f32[6,64]{1,0:T(8,128)S(1)}) fusion(f32[16,128]{1,0:T(8,128)S(1)} %bitcast.145, f32[6,64,16]{1,0,2:T(8,128)S(1)} %copy.85, bf16[6,64,1,16,128]{4,3,2,1,0:T(8,128)(2,1)S(1)} %copy-done.8, bf16[6,16,64,64]{3,2,1,0:T(8,128)(2,1)S(1)} %copy-done.9, f32[6,16,128,64]{2,3,0,1:T(8,128)} %fusion.9, ...), kind=kOutput, calls=%fused_computation.9 | convolution fusion | flops 106953984 | bytes 11832320 | tf_op jit(solution)/shard_map/nhqk,nkhd->nqhd/dot_general | solution.py:92
  167.7 0.1 mul.82
  167.8 14.1 %psum.29 = f32[64,16]{0,1:T(8,128)S(1)} all-reduce(f32[64,16]{0,1:T(8,128)S(1)} %get-tuple-element.11), channel_id=1, replica_groups=mesh['doc'=4,'seq'=8] {'seq'}, use_global_device_ids=true, to_apply=%region_6.7 | all-reduce | flops 1024 | bytes 8192 | tf_op jit(solution)/shard_map/psum | solution.py:121
  181.9 0.1 copy.68
  182.0 34.8 %all-reduce.4.cloned.1.call-done = f32[64,2048]{1,0:T(8,128)} async-done(((f32[64,2048]{1,0:T(8,128)}), f32[64,2048]{1,0:T(8,128)}) %all-reduce.4.cloned.1.call-update) | async-done | bytes 524304 | tf_op jit(solution)/shard_map/psum | solution.py:121
  216.7 0.2 div.43
  216.9 1.3 multiply_reduce_fusion.2
  218.3 0.3 convolution_reduce_fusion
  218.6 0.6 select_n.15
  (24 shorter events, 0.1 us)
Async XLA Ops:
  6.5 1.9 copy-start
  6.5 72.0 %all-reduce.6.cloned.1.call-start = ((), (), s32[]{:S(2)}) async-start(), calls=%async_computation.2 | async-start | bytes 1048576 | tf_op jit(solution)/shard_map/psum | solution.py:49
  8.6 1.7 copy-start.4
  10.3 5.5 %copy-start.1 = (bf16[384,2048]{1,0:T(8,128)(2,1)S(1)}, bf16[384,2048]{1,0:T(8,128)(2,1)}, u32[]{:S(2)}) copy-start(bf16[384,2048]{1,0:T(8,128)(2,1)} %param.6) | copy-start | bytes 4718596
  10.3 5.5 %copy-start.12 = (s32[64]{0:T(128)S(1)}, s32[64]{0:T(128)}, u32[]{:S(2)}) copy-start(s32[64]{0:T(128)} %param.8) | copy-start | bytes 772
  11.3 70.6 %collective-permute-start = (bf16[64,4096]{1,0:T(8,128)(2,1)}, bf16[64,4096]{1,0:T(8,128)(2,1)}, u32[]{:S(2)}, u32[]{:S(2)}) collective-permute-start(bf16[64,4096]{1,0:T(8,128)(2,1)} %get-tuple-element.25), channel_id=1, source_target_pairs={{0,1},{1,2},{2,3},{3,4},{4,5},{5,6},{6,7},{8,9},{9,10},{10,11},{11... | collective-permute-start | bytes 1572872 | tf_op jit(solution)/shard_map/ppermute | solution.py:15
  14.5 67.4 %collective-permute-start.1 = (bf16[64,4096]{1,0:T(8,128)(2,1)}, bf16[64,4096]{1,0:T(8,128)(2,1)}, u32[]{:S(2)}, u32[]{:S(2)}) collective-permute-start(bf16[64,4096]{1,0:T(8,128)(2,1)} %get-tuple-element.26), channel_id=1, source_target_pairs={{1,0},{2,1},{3,2},{4,3},{5,4},{6,5},{7,6},{9,8},{10,9},{11,10},{12... | collective-permute-start | bytes 1572872 | tf_op jit(solution)/shard_map/ppermute | solution.py:18
  16.2 2.1 copy-start.6
  18.3 122.1 %all-gather.3.cloned.1.call-start = ((), (), s32[]{:S(2)}) async-start(), calls=%async_computation.1 | async-start | bytes 2359296 | tf_op jit(solution)/shard_map/all_gather | solution.py:48
  19.5 197.2 %all-reduce.4.cloned.1.call-start = ((), (), s32[]{:S(2)}) async-start(), calls=%async_computation | async-start | bytes 1048576 | tf_op jit(solution)/shard_map/psum | solution.py:121
  78.5 3.4 %copy-start.5 = (bf16[384,4096]{1,0:T(8,128)(2,1)S(1)}, bf16[384,4096]{1,0:T(8,128)(2,1)}, u32[]{:S(2)}) copy-start(bf16[384,4096]{1,0:T(8,128)(2,1)} %copy-done.4) | copy-start | bytes 9437188
  90.8 2.6 %copy-start.7 = (f32[6,16,64,64]{3,2,1,0:T(8,128)S(1)}, f32[6,16,64,64]{3,2,1,0:T(8,128)}, u32[]{:S(2)}) copy-start(f32[6,16,64,64]{3,2,1,0:T(8,128)} %convolution_bitcast_fusion) | copy-start | bytes 4718596
  130.7 2.7 %copy-start.10 = (bf16[64,16,128]{2,0,1:T(8,128)(2,1)S(1)}, bf16[64,16,128]{2,0,1:T(8,128)(2,1)}, u32[]{:S(2)}) copy-start(bf16[64,16,128]{2,0,1:T(8,128)(2,1)} %get-tuple-element.10) | copy-start | bytes 786436
  140.4 2.1 copy-start.2
  143.4 1.2 copy-start.3
  159.1 3.0 %copy-start.9 = (bf16[6,16,64,64]{3,2,1,0:T(8,128)(2,1)S(1)}, bf16[6,16,64,64]{3,2,1,0:T(8,128)(2,1)}, u32[]{:S(2)}) copy-start(bf16[6,16,64,64]{3,2,1,0:T(8,128)(2,1)} %get-tuple-element.21) | copy-start | bytes 2359300
  161.3 1.6 copy-start.8
  161.3 1.6 copy-start.11
Sparse Core Ops, SparseCore 0:
  18.4 60.0 all-reduce.5
  80.2 28.1 all-gather.2
  162.3 54.4 all-reduce.3
